TPU v7x, 128 devices: a whole 4x4x4 slice. The times are simulated.
128 devices in a mesh: req: 4 (over y), tok: 32 (over z, x, core).
Axes of the slice: x: 4, y: 4, z: 4, core: 2. Of those that a mesh axis runs over, the one named last changes fastest.
Arguments:
- tokens: bfloat16 [8, 2048, 1536], P('req', 'tok'), may hold values from -16 to 16
- gain_attn: float32 [1536], replicated, may hold values from 0.1 to 1.9
- query_weight: bfloat16 [1536, 1536], replicated, may hold values from -0.375 to 0.375
- key_value_weight: bfloat16 [1536, 1024], replicated, may hold values from -0.15625 to 0.15625
- w_out: bfloat16 [1536, 1536], replicated, may hold values from -0.15625 to 0.15625
- kv_pool: bfloat16 [512, 64, 1024], P(('req', 'tok')), may hold values from -170 to 170, as said below
- migrate: int32 [512], P(('req', 'tok')), may hold values from 0 to 511, as said below
- page_table: int32 [8, 64], P('req'), may hold values from 0 to 127, as said below
- cache_len: int32 [8], P('req'), may hold values from 0 to 4096, as said below
- gain_ffn: float32 [1536], replicated, may hold values from 0.1 to 1.9
- routes: int32 [8, 2048, 8], P('req', 'tok'), may hold values from 0 to 31, all different within a row; in each aligned block of 64 rows (0 to 63, 64 to 127, ..., all dimensions but the last counted through in order) at most 24 rows name the same one
- gate_weights: float32 [8, 2048, 8], P('req', 'tok'), may hold values from 0.05 to 0.5
- w_gate_up: bfloat16 [32, 1536, 1024], P('tok'), may hold values from -0.15625 to 0.15625
- w_down: bfloat16 [32, 512, 1536], P('tok'), may hold values from -0.25 to 0.25
Outputs:
- attended: bfloat16 [8, 2048, 1536], P('req', 'tok')
- expert_mix: bfloat16 [8, 2048, 1536], P('req', 'tok')
Inputs may be any that keep to these rules, and one draw needn't show every extreme that they name: `kv_pool`: the values of the cached keys and values. `migrate`: A permutation of all slots that keeps a slot's tok index: slot a*128 + t*4 + i goes to some a2*128 + t*4 + i2. `page_table`: the rows of the 2 requests of one group together hold every slot of the group's pool exactly once. `cache_len`: each length lies within 128 of 0 or of 4096; some request has exactly 4096. `routes`: the 8 experts of a token differ; in each aligned block of 64 rows (one request's tokens on one device) no expert is named more than 24 times.
All inputs are finite; a program needn't handle non-finite values.
Results may differ from a plain program's by a relative error of at most 0.025.
Values may be sent and summed in bfloat16 or wider, within the bound.
No kernel may reach another device: no remote copies, remote signals or barrier semaphores. Data moves between devices by JAX's collectives and lax.ppermute only.
A program may use at most 192 MiB of HBM per device.

v0:
```python
import jax
import jax.numpy as jnp
from jax import lax
from jax.sharding import PartitionSpec as P

QUERY_HEADS = 24
KEY_VALUE_HEADS = 8
HEAD_SIZE = 64
FF = 512
TOPK = 8
MOST = 24
score_masked = -1e30
epsilon = 1e-06
far_position = 1 << 30


def rms_norm(values, gain_vec):
    widened = values.astype(jnp.float32)
    inverse = lax.rsqrt(jnp.mean(widened * widened, axis=-1, keepdims=True) + epsilon)
    return (widened * inverse * gain_vec).astype(jnp.bfloat16)


def pick_block(row_total):
    block_len = min(row_total, 1024)
    while row_total % block_len:
        block_len -= 1
    return block_len


def attend(running, head_rows, meta_abs, query_heads, query_abs):
    row_total = head_rows.shape[1]
    block_len = pick_block(row_total)
    blocks = row_total // block_len
    heads_kv = query_heads.shape[0]
    head_dim = query_heads.shape[2]

    def loop_step(index, carried):
        run_max, run_sum, run_acc = carried
        block = lax.dynamic_slice_in_dim(head_rows, index * block_len, block_len, 1)
        abs_block = lax.dynamic_slice_in_dim(meta_abs, index * block_len, block_len, 0)
        visible = (abs_block[None, :] <= query_abs[:, None])[None, :, :]
        scores = jnp.einsum(
            "hqd,hkd->hqk", query_heads, block[:heads_kv], preferred_element_type=jnp.float32
        ) * head_dim ** (-0.5)
        scores = jnp.where(visible, scores, score_masked)
        new_max = jnp.maximum(run_max, jnp.max(scores, axis=-1))
        weight = jnp.where(visible, jnp.exp(scores - new_max[..., None]), 0.0)
        factor = jnp.exp(run_max - new_max)
        run_sum = run_sum * factor + jnp.sum(weight, axis=-1)
        update = jnp.einsum(
            "hqk,hkd->hqd",
            weight.astype(jnp.bfloat16),
            block[heads_kv:],
            preferred_element_type=jnp.float32,
        )
        run_acc = run_acc * factor[..., None] + update
        return (new_max, run_sum, run_acc)

    return lax.fori_loop(0, blocks, loop_step, running)


def pick_member(state, member_id):
    return jax.tree.map(lambda array: array[member_id], state)


def stack_members(states):
    return jax.tree.map(lambda *arrays: jnp.stack(arrays), *states)


def local(
    tokens,
    gain_attn,
    query_weight,
    key_value_weight,
    w_out,
    kv_pool,
    migrate,
    page_table,
    cache_len,
    gain_ffn,
    routes,
    gate_weights,
    w_gate_up,
    w_down,
):
    request_per_shard, tokens_per_shard, model_width = tokens.shape
    local_rows = request_per_shard * tokens_per_shard
    tok_count = lax.axis_size("tok")
    req_count = lax.axis_size("req")
    tok_index = lax.axis_index("tok")
    kv_width = key_value_weight.shape[1]
    groups_per_head = QUERY_HEADS // KEY_VALUE_HEADS
    flat_rows = tokens.reshape(local_rows, model_width)
    normalized_input = rms_norm(flat_rows, gain_attn)
    query_rows = (
        jnp.dot(normalized_input, query_weight, preferred_element_type=jnp.float32)
        .astype(jnp.bfloat16)
        .reshape(request_per_shard, tokens_per_shard, KEY_VALUE_HEADS, groups_per_head, HEAD_SIZE)
    )
    query_heads = query_rows.transpose(0, 2, 3, 1, 4).reshape(
        request_per_shard, KEY_VALUE_HEADS, groups_per_head * tokens_per_shard, HEAD_SIZE
    )
    keyval_pos = (
        jnp.einsum(
            "rcd,dk->crk",
            normalized_input.reshape(request_per_shard, tokens_per_shard, model_width),
            key_value_weight,
            preferred_element_type=jnp.float32,
        )
        .astype(jnp.bfloat16)
        .reshape(tokens_per_shard, request_per_shard * kv_width)
    )
    span_pos = jnp.arange(tokens_per_shard, dtype=jnp.int32)
    query_abs = cache_len[:, None] + tok_index * tokens_per_shard + span_pos[None, :]
    query_abs_rep = jnp.tile(query_abs, (1, groups_per_head))
    pages_dev = kv_pool.shape[0]
    page_rows = kv_pool.shape[1]
    pages_req = page_table.shape[1]
    slots_all = request_per_shard * pages_req
    cache_pos = jnp.arange(pages_req * page_rows, dtype=jnp.int32)
    target = migrate // slots_all * pages_dev + migrate % pages_dev
    places = jnp.arange(req_count * pages_dev, dtype=jnp.int32)
    route_pages = (places[:, None] == target[None, :]).astype(jnp.bfloat16)
    outgoing = jnp.einsum(
        "sp,prk->srk", route_pages, kv_pool, preferred_element_type=jnp.float32
    ).astype(jnp.bfloat16)
    outgoing = outgoing.reshape(req_count, pages_dev, page_rows, kv_width)
    arrived = lax.all_to_all(outgoing, "req", split_axis=0, concat_axis=0, tiled=True)
    migrated = jnp.sum(arrived, axis=0, dtype=jnp.float32).astype(jnp.bfloat16)
    query_count = groups_per_head * tokens_per_shard
    start_state = (
        jnp.full((request_per_shard, KEY_VALUE_HEADS, query_count), score_masked, jnp.float32),
        jnp.zeros((request_per_shard, KEY_VALUE_HEADS, query_count), jnp.float32),
        jnp.zeros((request_per_shard, KEY_VALUE_HEADS, query_count, HEAD_SIZE), jnp.float32),
    )
    pool_all = lax.all_gather(migrated, "tok", axis=0, tiled=True)
    pool_heads = pool_all.reshape(
        pool_all.shape[0], page_rows, 2 * KEY_VALUE_HEADS, HEAD_SIZE
    ).transpose(2, 0, 1, 3)
    results = []
    for member_id in range(request_per_shard):
        rows = jnp.take(pool_heads, page_table[member_id], axis=1).reshape(
            2 * KEY_VALUE_HEADS, pages_req * page_rows, HEAD_SIZE
        )
        cache_abs = jnp.where(cache_pos < cache_len[member_id], cache_pos, far_position)
        results.append(
            attend(
                pick_member(start_state, member_id),
                rows,
                cache_abs,
                query_heads[member_id],
                query_abs_rep[member_id],
            )
        )
    running = stack_members(results)
    piece = lax.all_gather(keyval_pos, "tok", axis=0, tiled=True)
    row_total = piece.shape[0]
    by_member = piece.reshape(
        row_total, request_per_shard, 2 * KEY_VALUE_HEADS, HEAD_SIZE
    ).transpose(1, 2, 0, 3)
    positions = jnp.arange(row_total, dtype=jnp.int32)
    fold_results = []
    for member_id in range(request_per_shard):
        piece_abs = cache_len[member_id] + positions
        fold_results.append(
            attend(
                pick_member(running, member_id),
                by_member[member_id],
                piece_abs,
                query_heads[member_id],
                query_abs_rep[member_id],
            )
        )
    final_state = stack_members(fold_results)
    run_max, run_sum, run_acc = final_state
    normalized_heads = (
        (run_acc / run_sum[..., None])
        .astype(jnp.bfloat16)
        .reshape(request_per_shard, KEY_VALUE_HEADS, groups_per_head, tokens_per_shard, HEAD_SIZE)
    )
    heads_out = normalized_heads.transpose(0, 3, 1, 2, 4).reshape(
        local_rows, QUERY_HEADS * HEAD_SIZE
    )
    projected = jnp.dot(heads_out, w_out, preferred_element_type=jnp.float32)
    attended = projected.astype(jnp.bfloat16)
    residual = (flat_rows.astype(jnp.float32) + projected).astype(jnp.bfloat16)
    normed_ffn = rms_norm(residual, gain_ffn)
    member = jnp.arange(request_per_shard, dtype=jnp.int32)
    experts_total = tok_count * w_gate_up.shape[0]
    route_local = routes.reshape(request_per_shard, tokens_per_shard * TOPK)
    onehot = route_local[..., None] == jnp.arange(experts_total, dtype=jnp.int32)[None, None, :]
    rank_all = jnp.cumsum(onehot.astype(jnp.int32), axis=1) - 1
    rank_of = jnp.sum(jnp.where(onehot, rank_all, 0), axis=2)
    slot_of = route_local * (request_per_shard * MOST) + member[:, None] * MOST + rank_of
    slot_flat = slot_of.reshape(-1)
    capacity = experts_total * request_per_shard * MOST
    token_ids = jnp.arange(local_rows * TOPK, dtype=jnp.int32) // TOPK
    source = jnp.zeros((capacity,), jnp.int32).at[slot_flat].set(token_ids + 1)
    gathered = jnp.take(normed_ffn, jnp.maximum(source - 1, 0), axis=0)
    outbound = jnp.where((source > 0)[:, None], gathered, jnp.zeros_like(gathered)).reshape(
        experts_total, request_per_shard * MOST, model_width
    )
    inbound = lax.all_to_all(outbound, "tok", split_axis=0, concat_axis=1, tiled=True)
    gate_up = jnp.einsum("erd,edf->erf", inbound, w_gate_up, preferred_element_type=jnp.float32)
    hidden = (jax.nn.silu(gate_up[..., :FF]) * gate_up[..., FF:]).astype(jnp.bfloat16)
    expert_out = jnp.einsum(
        "erf,efd->erd", hidden, w_down, preferred_element_type=jnp.float32
    ).astype(jnp.bfloat16)
    returned = lax.all_to_all(expert_out, "tok", split_axis=1, concat_axis=0, tiled=True)
    picked = jnp.take(returned.reshape(capacity, model_width), slot_flat, axis=0).reshape(
        local_rows, TOPK, model_width
    )
    mixture = jnp.einsum(
        "qk,qkd->qd", gate_weights.reshape(local_rows, TOPK), picked.astype(jnp.float32)
    )
    return (
        attended.reshape(request_per_shard, tokens_per_shard, model_width),
        mixture.astype(jnp.bfloat16).reshape(request_per_shard, tokens_per_shard, model_width),
    )


def solution(mesh):
    placed = (
        P("req", "tok", None),
        P(),
        P(),
        P(),
        P(),
        P(("req", "tok"), None, None),
        P(("req", "tok")),
        P("req", None),
        P("req"),
        P(),
        P("req", "tok", None),
        P("req", "tok", None),
        P("tok", None, None),
        P("tok", None, None),
    )
    return jax.shard_map(
        local,
        mesh=mesh,
        in_specs=placed,
        out_specs=(P("req", "tok", None), P("req", "tok", None)),
        check_vma=False,
    )
```

profile of v0, /device:TPU:0, one launch (start us, length us, event | category | flops | bytes accessed | tf_op | source)
XLA Modules:
  0.0 831.7 jit_solution(13190696790973247134)
XLA Ops:
  12.0 3.2 convolution_convert_fusion.2
  15.3 4.1 reshape.408
  21.8 30.8 %all_to_all.23 = bf16[4,4,64,1024]{3,1,2,0:T(4,128)(2,1)} all-to-all(bf16[4,4,64,1024]{3,1,2,0:T(4,128)(2,1)S(1)} %copy.95), channel_id=1, replica_groups=mesh['req'=4,'tok'=32] {'req'}, dimensions={0} | all-to-all | bytes 4194304 | tf_op jit(solution)/shard_map/all_to_all | solution.py:128
  52.6 3.7 reduce_sum.95
  64.4 4.0 convolution_convert_fusion.1
  70.8 5.2 fusion.125
  88.1 4.5 scatter_custom_fusion
  101.6 12.4 %copy.105 = bf16[2048,2048]{0,1:T(8,128)(2,1)} copy(bf16[2048,2048]{1,0:T(8,128)(2,1)} %all-gather.5.cloned.1.call-done) | data formatting | bytes 16777216 | tf_op jit(solution)/shard_map/all_gather | solution.py:156
  114.0 6.4 slice_bitcast_fusion.1
  120.4 21.6 %all-gather.3.cloned.1.call-done = bf16[128,64,1024]{2,1,0:T(8,128)(2,1)} async-done(((bf16[4,64,1024]{2,1,0:T(8,128)(2,1)}), bf16[128,64,1024]{2,1,0:T(8,128)(2,1)}) %all-gather.3.cloned.1.call-update) | async-done | bytes 16777232 | tf_op jit(solution)/shard_map/all_gather | solution.py:136
  142.0 23.0 %copy.98 = bf16[128,64,1024]{0,2,1:T(8,128)(2,1)} copy(bf16[128,64,1024]{2,1,0:T(8,128)(2,1)} %all-gather.3.cloned.1.call-done) | data formatting | bytes 33554432 | tf_op jit(solution)/shard_map/all_gather | solution.py:136
  165.1 46.1 %copy.99 = bf16[128,64,16,64]{3,1,0,2:T(8,128)(2,1)} copy(bf16[128,64,16,64]{0,3,2,1:T(8,128)(2,1)} %bitcast.228) | data formatting | bytes 33554432 | tf_op jit(solution)/shard_map/reshape | solution.py:137
  211.1 11.9 %gather_fusion.2 = bf16[64,16,64,64]{3,2,1,0:T(8,128)(2,1)} fusion(bf16[16,128,64,64]{3,2,1,0:T(8,128)(2,1)} %bitcast.226, s32[1024]{0:T(1024)S(1)} %pad_clamp_fusion.2), kind=kCustom, calls=%fused_computation.clone | custom fusion | bytes 16777472 | tf_op jit(solution)/shard_map/jit(_take)/gather | solution.py:142
  223.0 11.9 %gather_fusion.3 = bf16[64,16,64,64]{3,2,1,0:T(8,128)(2,1)} fusion(bf16[16,128,64,64]{3,2,1,0:T(8,128)(2,1)} %bitcast.227, s32[1024]{0:T(1024)S(1)} %pad_clamp_fusion.1), kind=kCustom, calls=%fused_computation.1.clone | custom fusion | bytes 16777472 | tf_op jit(solution)/shard_map/jit(_take)/gather | solution.py:142
  234.9 23.0 %select_bitcast_fusion = (bf16[16,64,64,64]{3,2,0,1:T(8,128)(2,1)}, bf16[16,64,64,64]{3,2,0,1:T(8,128)(2,1)}) fusion(bf16[64,16,64,64]{3,2,1,0:T(8,128)(2,1)} %gather_fusion.3, pred[64]{0:T(512)(128)(4,1)S(1)} %get-tuple-element.895, bf16[64,16,64,64]{3,2,1,0:T(8,128)(2,1)} %gather_fusion.2, pred[64]{0:T(512)(128)(4,1)S(1)} %get-tuple-element.873), kind=kLoop, calls=%fused_computation.91 | loop fusion | flops 8388608 | bytes 33554560 | tf_op jit(solution)/shard_map/jit(_take)/select_n | solution.py:142
  257.9 22.9 %copy.100 = bf16[16,64,64,64]{2,1,3,0:T(8,128)(2,1)} copy(bf16[16,64,64,64]{3,2,0,1:T(8,128)(2,1)} %get-tuple-element.902) | data formatting | bytes 16777216 | tf_op jit(solution)/shard_map/jit(_take)/select_n | solution.py:142
  280.7 22.6 %reshape.410 = bf16[16,4096,64]{1,2,0:T(8,128)(2,1)} reshape(bf16[16,64,64,64]{2,1,3,0:T(8,128)(2,1)} %copy.100) | data formatting | bytes 16777216 | tf_op jit(solution)/shard_map/reshape | solution.py:142
  303.3 60.5 %while.74 = (s32[]{:T(128)}, f32[8,192]{1,0:T(8,128)S(1)}, f32[8,192]{1,0:T(8,128)S(1)}, f32[8,192,64]{1,2,0:T(8,128)}, s32[4096]{0:T(1024)S(1)}, /*index=5*/bf1...) while((s32[]{:T(128)}, f32[8,192]{1,0:T(8,128)S(1)}, ...), condition=%wide.region_5.7_spmd.clone, body=%wide.region_2.6_spmd.clone.sunk | while | flops 423599616 | bytes 24100308 | solution.py:59
  303.6 5.2 fusion.178
  308.8 3.9 fusion.179
  312.8 5.6 fusion.181
  318.6 5.2 fusion.178
  323.9 3.9 fusion.179
  327.8 5.7 fusion.181
  333.8 5.2 fusion.178
  339.0 3.9 fusion.179
  343.0 5.7 fusion.181
  349.0 5.2 fusion.178
  354.2 3.9 fusion.179
  358.1 5.7 fusion.181
  363.9 27.0 %while.72 = (s32[]{:T(128)}, f32[8,192]{1,0:T(8,128)S(1)}, f32[8,192]{1,0:T(8,128)S(1)}, f32[8,192,64]{1,2,0:T(8,128)}, s32[2048]{0:T(1024)S(1)}, /*index=5*/bf1...) while((s32[]{:T(128)}, f32[8,192]{1,0:T(8,128)S(1)}, ...), condition=%wide.region_9.11_spmd.clone, body=%wide.region_6.10_spmd.clone.sunk | while | flops 423496704 | bytes 49266148 | solution.py:59
  371.8 5.7 fusion.168
  385.1 5.7 fusion.168
  391.5 22.9 %copy.108 = bf16[16,64,64,64]{2,1,3,0:T(8,128)(2,1)} copy(bf16[16,64,64,64]{3,2,0,1:T(8,128)(2,1)} %get-tuple-element.901) | data formatting | bytes 16777216 | tf_op jit(solution)/shard_map/jit(_take)/select_n | solution.py:142
  414.4 22.6 %reshape.414 = bf16[16,4096,64]{1,2,0:T(8,128)(2,1)} reshape(bf16[16,64,64,64]{2,1,3,0:T(8,128)(2,1)} %copy.108) | data formatting | bytes 16777216 | tf_op jit(solution)/shard_map/reshape | solution.py:142
  437.0 63.0 %while.75 = (s32[]{:T(128)}, f32[8,192]{1,0:T(8,128)S(1)}, f32[8,192]{1,0:T(8,128)S(1)}, f32[8,192,64]{1,2,0:T(8,128)}, s32[4096]{0:T(1024)}, /*index=5*/bf16[16...) while((s32[]{:T(128)}, f32[8,192]{1,0:T(8,128)S(1)}, ...), condition=%wide.region_13.15_spmd.clone, body=%wide.region_10.14_spmd.clone.sunk | while | flops 423599616 | bytes 24100308 | solution.py:59
  438.0 5.2 fusion.185
  443.2 3.9 fusion.186
  447.1 5.6 fusion.188
  453.6 5.2 fusion.185
  458.8 3.9 fusion.186
  462.7 5.7 fusion.188
  469.4 5.2 fusion.185
  474.6 3.9 fusion.186
  478.5 5.7 fusion.188
  485.2 5.2 fusion.185
  490.4 3.9 fusion.186
  494.3 5.7 fusion.188
  500.0 27.1 %while.73 = (s32[]{:T(128)}, f32[8,192]{1,0:T(8,128)S(1)}, f32[8,192]{1,0:T(8,128)S(1)}, f32[8,192,64]{1,2,0:T(8,128)}, s32[2048]{0:T(1024)S(1)}, /*index=5*/bf1...) while((s32[]{:T(128)}, f32[8,192]{1,0:T(8,128)S(1)}, ...), condition=%wide.region_17.19_spmd.clone, body=%wide.region_14.18_spmd.clone.sunk | while | flops 423496704 | bytes 49266148 | solution.py:59
  508.1 5.7 fusion.174
  521.5 5.7 fusion.174
  535.8 3.0 copy.113
  541.6 3.4 fusion.96
  545.9 6.2 gather_fusion
  554.9 62.1 %all_to_all.24 = bf16[32,48,1536]{2,1,0:T(8,128)(2,1)S(1)} all-to-all(bf16[32,48,1536]{2,1,0:T(8,128)(2,1)S(1)} %select_select_fusion), channel_id=1, replica_groups=mesh['req'=4,'tok'=32] {'tok'}, dimensions={0} | all-to-all | bytes 9437184 | tf_op jit(solution)/shard_map/all_to_all | solution.py:203
  617.0 5.4 convolution_bitcast_fusion
  625.3 52.2 %copy.141 = bf16[1,1536,1536]{2,0,1:T(2,128)(2,1)} copy(bf16[1,1536,1536]{2,1,0:T(8,128)(2,1)S(1)} %fusion.78) | data formatting | bytes 9437184 | tf_op jit(solution)/shard_map/convert_element_type | solution.py:208
  678.1 32.0 %reduce.4 = bf16[1536,1536]{1,0:T(8,128)(2,1)} reduce(bf16[1536,1,1536]{2,1,0:T(2,128)(2,1)} %bitcast.229, bf16[]{:T(256)} %broadcast.485), dimensions={1}, to_apply=%bitcast.192.reduce_sub_computation | reduce | bytes 9437186
  710.0 8.2 reshape.485
  718.3 5.2 all-to-all-start.2
  724.2 59.0 %all-to-all-done.2 = bf16[32,2,36864]{2,1,0:T(2,128)(2,1)} async-done(((bf16[32,2,36864]{2,1,0:T(2,128)(2,1)}), bf16[32,2,36864]{2,1,0:T(2,128)(2,1)}, u32[]{:S(2)}, u32[]{:S(2)}) %all-to-all-start.2) | async-done | bytes 4718624 | tf_op jit(solution)/shard_map/all_to_all | solution.py:209
  783.2 20.2 %reshape.486 = bf16[1536,1,1536]{2,1,0:T(2,128)(2,1)} reshape(bf16[32,2,36864]{2,1,0:T(2,128)(2,1)} %all-to-all-done.2) | data formatting | bytes 9437184
  803.4 7.2 copy.139
  810.7 10.2 %gather_fusion.1 = bf16[1024,1536]{1,0:T(8,128)(2,1)} fusion(bf16[1536,1536]{1,0:T(8,128)(2,1)} %bitcast.225, s32[1024]{0:T(1024)S(1)} %broadcast_clamp_fusion), kind=kCustom, calls=%fused_computation.3 | custom fusion | bytes 6295552 | tf_op jit(solution)/shard_map/jit(_take)/gather | solution.py:210
  (230 shorter events, 97.9 us)
Async XLA Ops:
  7.2 609.8 %copy-start = (bf16[1,1536,1024]{2,1,0:T(8,128)(2,1)S(1)}, bf16[1,1536,1024]{2,1,0:T(8,128)(2,1)}, u32[]{:S(2)}) copy-start(bf16[1,1536,1024]{2,1,0:T(8,128)(2,1)} %param.36) | copy-start | bytes 9437188
  7.2 4.8 copy-start.24
  7.2 94.4 %all-gather.5.cloned.1.call-start = ((), (), s32[]{:S(2)}) async-start(), calls=%async_computation.4 | async-start | bytes 8650752 | tf_op jit(solution)/shard_map/all_gather | solution.py:156
  12.0 130.0 %all-gather.3.cloned.1.call-start = ((), (), s32[]{:S(2)}) async-start(), calls=%async_computation.3 | async-start | bytes 17301504 | tf_op jit(solution)/shard_map/all_gather | solution.py:136
  19.4 44.1 %copy-start.3 = (bf16[2,64,1536]{2,1,0:T(8,128)(2,1)S(1)}, bf16[2,64,1536]{2,1,0:T(8,128)(2,1)}, u32[]{:S(2)}) copy-start(bf16[2,64,1536]{2,1,0:T(8,128)(2,1)} %param.24) | copy-start | bytes 1179652
  86.4 27.6 %copy-start.12 = (s32[2,512]{1,0:T(2,128)}, s32[2,512]{1,0:T(2,128)S(1)}, u32[]{:S(2)}) copy-start(s32[2,512]{1,0:T(2,128)S(1)} %fusion.111) | copy-start | bytes 12292
  87.2 26.9 %copy-start.9 = (s32[2,64,8]{1,2,0:T(8,128)}, s32[2,64,8]{1,2,0:T(8,128)S(1)}, u32[]{:S(2)}) copy-start(s32[2,64,8]{1,2,0:T(8,128)S(1)} %broadcast_multiply_fusion) | copy-start | bytes 12292
  87.4 0.6 copy-start.21
  88.0 26.0 %copy-start.17 = (s32[1024,1]{0,1:T(1,128)}, s32[1024,1]{0,1:T(1,128)S(1)}, u32[]{:S(2)}) copy-start(s32[1024,1]{0,1:T(1,128)S(1)} %compare_select_fusion) | copy-start | bytes 12292
  367.0 2.7 copy-start.1
  380.4 2.7 copy-start.1
  414.4 22.6 %copy-start.6 = (f32[8,192]{1,0:T(8,128)S(1)}, f32[8,192]{1,0:T(8,128)}, u32[]{:S(2)}) copy-start(f32[8,192]{1,0:T(8,128)} %custom-call.3) | copy-start | bytes 18436
  414.4 22.6 %copy-start.7 = (f32[8,192]{1,0:T(8,128)S(1)}, f32[8,192]{1,0:T(8,128)}, u32[]{:S(2)}) copy-start(f32[8,192]{1,0:T(8,128)} %custom-call.4) | copy-start | bytes 18436
  414.4 22.6 %copy-start.11 = (s32[64]{0:T(128)S(1)}, s32[64]{0:T(128)}, u32[]{:S(2)}) copy-start(s32[64]{0:T(128)} %get-tuple-element.1177) | copy-start | bytes 772
  437.0 63.0 %copy-start.8 = (s32[2048]{0:T(1024)S(1)}, s32[2048]{0:T(1024)}, u32[]{:S(2)}) copy-start(s32[2048]{0:T(1024)} %iota_add_fusion) | copy-start | bytes 24580
  503.3 2.7 copy-start.2
  516.7 2.7 copy-start.2
  527.1 14.4 %copy-start.4 = (bf16[2,64,1536]{2,1,0:T(8,128)(2,1)S(1)}, bf16[2,64,1536]{2,1,0:T(8,128)(2,1)}, u32[]{:S(2)}) copy-start(bf16[2,64,1536]{2,1,0:T(8,128)(2,1)} %param.24) | copy-start | bytes 1179652
  530.0 15.0 %copy-start.19 = (f32[1536]{0:T(1024)S(1)}, f32[1536]{0:T(1024)}, u32[]{:S(2)}) copy-start(f32[1536]{0:T(1024)} %param.33) | copy-start | bytes 18436
  533.0 12.9 %copy-start.14 = (s32[2048]{0:T(1024)S(1)}, s32[2048]{0:T(1024)}, u32[]{:S(2)}) copy-start(s32[2048]{0:T(1024)} %pad_clamp_fusion) | copy-start | bytes 24580
  541.6 3.4 copy-start.5
  545.9 6.2 copy-start.15
  545.9 6.2 copy-start.16
  617.0 5.4 copy-start.23
  718.3 5.2 copy-start.13
  718.3 5.4 copy-start.10
  718.3 5.5 copy-start.22
  718.3 5.8 copy-start.20
  718.3 5.9 copy-start.18
  718.3 64.9 %all-to-all-start.2 = ((bf16[32,2,36864]{2,1,0:T(2,128)(2,1)}), bf16[32,2,36864]{2,1,0:T(2,128)(2,1)}, u32[]{:S(2)}, u32[]{:S(2)}) async-start(bf16[32,2,36864]{2,1,0:T(2,128)(2,1)} %reshape.485), calls=%async_computation.2 | async-start | bytes 9437184 | tf_op jit(solution)/shard_map/all_to_all | solution.py:209
Sparse Core Ops, SparseCore 0:
  12.1 55.4 all-gather.4
  69.9 72.0 all-gather.2
where the time goes:
time: 845 us; the launch traced here: 832 us
  local copies, waits for them, and re-layouts  372 us (44%)
  matrix products  145 us (17%)
  other arithmetic  120 us (14%)
  blocking collectives  92.9 us (11%)
  waiting for transfers between devices  80.6 us (10%)
  between operations  14.7 us (2%)
    dot_general x12, matrix products, loop_step(): jnp.einsum('hqk,hkd->hqd', weight.astype(jnp.bfloat16), block[heads_kv:],...  68.1 us
    all_to_all x1, blocking collectives, local(): lax.all_to_all(outbound, 'tok', split_axis=0, concat_axis=1, tiled=True)  62.1 us
    all_to_all x1, waiting for transfers between devices, local(): lax.all_to_all(expert_out, 'tok', split_axis=1, concat_axis=0, tiled=True)  59 us
    convert_element_type x1, local copies, waits for them, and re-layouts, local(): expert_out = jnp.einsum('erf,efd->erd', hidden, w_down, preferred_element...  52.2 us
    dot_general x12, matrix products, loop_step(): jnp.einsum('hqd,hkd->hqk', query_heads, block[:heads_kv], preferred_eleme...  52.2 us
    reshape x1, local copies, waits for them, and re-layouts, local(): pool_all.reshape(pool_all.shape[0], page_rows, 2 * KEY_VALUE_HEADS, HEAD_...  46.1 us
    select_n x2, local copies, waits for them, and re-layouts, local(): jnp.take(pool_heads, page_table[member_id], axis=1)  45.8 us
    reshape x2, local copies, waits for them, and re-layouts, local(): jnp.take(pool_heads, page_table[member_id], axis=1)  45.2 us
  transfers between devices with their start and end apart: 3, of which 2 were waited for; matrix products, arithmetic and copies ran while one was open for 9% of the time, Pallas kernels for 0%

commit v1 on v0

--- a/solution.py
+++ b/solution.py
@@ -12,6 +12,13 @@
 score_masked = -1e30
 epsilon = 1e-06
 far_position = 1 << 30
+
+
+def swap_blocks(x, mesh_axis, split, join):
+    size = lax.axis_size(mesh_axis)
+    tiles = jnp.stack(jnp.split(x, size, axis=split), axis=0)
+    tiles = lax.all_to_all(tiles, mesh_axis, split_axis=0, concat_axis=0)
+    return jnp.concatenate(tiles, axis=join)
 
 
 def rms_norm(values, gain_vec):
@@ -206,7 +213,7 @@
     expert_out = jnp.einsum(
         "erf,efd->erd", hidden, w_down, preferred_element_type=jnp.float32
     ).astype(jnp.bfloat16)
-    returned = lax.all_to_all(expert_out, "tok", split_axis=1, concat_axis=0, tiled=True)
+    returned = swap_blocks(expert_out, "tok", 1, 0)
     picked = jnp.take(returned.reshape(capacity, model_width), slot_flat, axis=0).reshape(
         local_rows, TOPK, model_width
     )

time: 845 us -> 745 us (0.88)
  local copies, waits for them, and re-layouts: 372 us -> 305 us
  other arithmetic: 120 us -> 88.3 us
    convert_element_type x1 -> x0, local copies, waits for them, and re-layouts: 52.2 us -> none  [local(): expert_out = jnp.einsum('erf,efd->erd', hidden, w_down, preferred_element...]
    unnamed x7 -> x6, other arithmetic: 32 us -> 0.01 us
    unnamed x56 -> x83, local copies, waits for them, and re-layouts: 40.1 us -> 24.7 us
  transfers between devices with their start and end apart: 3 -> 3, of which waited for: 2 -> 2; matrix products, arithmetic and copies ran while one was open for 9% -> 11% of each run, Pallas kernels for 0% -> 0%
where the time goes in v1:
time: 745 us; the launch traced here: 732 us
  local copies, waits for them, and re-layouts  305 us (41%)
  matrix products  145 us (19%)
  blocking collectives  93 us (12%)
  other arithmetic  88.3 us (12%)
  waiting for transfers between devices  80.5 us (11%)
  between operations  14.6 us (2%)
    dot_general x12, matrix products, loop_step(): jnp.einsum('hqk,hkd->hqd', weight.astype(jnp.bfloat16), block[heads_kv:],...  68.1 us
    all_to_all x1, blocking collectives, local(): lax.all_to_all(outbound, 'tok', split_axis=0, concat_axis=1, tiled=True)  62.1 us
    all_to_all x1, waiting for transfers between devices, swap_blocks(): tiles = lax.all_to_all(tiles, mesh_axis, split_axis=0, concat_axis=0)  59 us
    dot_general x12, matrix products, loop_step(): jnp.einsum('hqd,hkd->hqk', query_heads, block[:heads_kv], preferred_eleme...  52.2 us
    reshape x1, local copies, waits for them, and re-layouts, local(): pool_all.reshape(pool_all.shape[0], page_rows, 2 * KEY_VALUE_HEADS, HEAD_...  46.1 us
    select_n x2, local copies, waits for them, and re-layouts, local(): jnp.take(pool_heads, page_table[member_id], axis=1)  45.7 us
    reshape x2, local copies, waits for them, and re-layouts, local(): jnp.take(pool_heads, page_table[member_id], axis=1)  45.1 us
    reduce_sum x12, other arithmetic, loop_step(): run_sum = run_sum * factor + jnp.sum(weight, axis=-1)  39.6 us
  transfers between devices with their start and end apart: 3, of which 2 were waited for; matrix products, arithmetic and copies ran while one was open for 11% of the time, Pallas kernels for 0%

profile of v1, /device:TPU:0, one launch (start us, length us, event | category | flops | bytes accessed | tf_op | source)
XLA Modules:
  0.0 732.3 jit_solution(8099548670011313187)
XLA Ops:
  12.1 3.3 convolution_convert_fusion.2
  15.3 4.1 reshape.401
  21.8 30.9 %all_to_all.19 = bf16[4,4,64,1024]{3,1,2,0:T(4,128)(2,1)} all-to-all(bf16[4,4,64,1024]{3,1,2,0:T(4,128)(2,1)S(1)} %copy.66), channel_id=1, replica_groups=mesh['req'=4,'tok'=32] {'req'}, dimensions={0} | all-to-all | bytes 4194304 | tf_op jit(solution)/shard_map/all_to_all | solution.py:135
  52.7 3.7 reduce_sum.95
  64.5 4.0 convolution_convert_fusion.1
  70.9 5.2 fusion.157
  88.2 4.5 scatter_custom_fusion
  101.7 12.5 %copy.76 = bf16[2048,2048]{0,1:T(8,128)(2,1)} copy(bf16[2048,2048]{1,0:T(8,128)(2,1)} %all-gather.5.cloned.1.call-done) | data formatting | bytes 16777216 | tf_op jit(solution)/shard_map/all_gather | solution.py:163
  114.2 6.4 slice_bitcast_fusion.1
  120.6 21.4 %all-gather.3.cloned.1.call-done = bf16[128,64,1024]{2,1,0:T(8,128)(2,1)} async-done(((bf16[4,64,1024]{2,1,0:T(8,128)(2,1)}), bf16[128,64,1024]{2,1,0:T(8,128)(2,1)}) %all-gather.3.cloned.1.call-update) | async-done | bytes 16777232 | tf_op jit(solution)/shard_map/all_gather | solution.py:143
  142.0 23.0 %copy.69 = bf16[128,64,1024]{0,2,1:T(8,128)(2,1)} copy(bf16[128,64,1024]{2,1,0:T(8,128)(2,1)} %all-gather.3.cloned.1.call-done) | data formatting | bytes 33554432 | tf_op jit(solution)/shard_map/all_gather | solution.py:143
  165.0 46.1 %copy.70 = bf16[128,64,16,64]{3,1,0,2:T(8,128)(2,1)} copy(bf16[128,64,16,64]{0,3,2,1:T(8,128)(2,1)} %bitcast.349) | data formatting | bytes 33554432 | tf_op jit(solution)/shard_map/reshape | solution.py:144
  211.0 11.9 %gather_fusion.2 = bf16[64,16,64,64]{3,2,1,0:T(8,128)(2,1)} fusion(bf16[16,128,64,64]{3,2,1,0:T(8,128)(2,1)} %bitcast.347, s32[1024]{0:T(1024)S(1)} %pad_clamp_fusion.2), kind=kCustom, calls=%fused_computation.clone | custom fusion | bytes 16777472 | tf_op jit(solution)/shard_map/jit(_take)/gather | solution.py:149
  222.9 11.9 %gather_fusion.3 = bf16[64,16,64,64]{3,2,1,0:T(8,128)(2,1)} fusion(bf16[16,128,64,64]{3,2,1,0:T(8,128)(2,1)} %bitcast.348, s32[1024]{0:T(1024)S(1)} %pad_clamp_fusion.1), kind=kCustom, calls=%fused_computation.1.clone | custom fusion | bytes 16777472 | tf_op jit(solution)/shard_map/jit(_take)/gather | solution.py:149
  234.8 23.0 %select_bitcast_fusion = (bf16[16,64,64,64]{3,2,0,1:T(8,128)(2,1)}, bf16[16,64,64,64]{3,2,0,1:T(8,128)(2,1)}) fusion(bf16[64,16,64,64]{3,2,1,0:T(8,128)(2,1)} %gather_fusion.3, pred[64]{0:T(512)(128)(4,1)S(1)} %get-tuple-element.863, bf16[64,16,64,64]{3,2,1,0:T(8,128)(2,1)} %gather_fusion.2, pred[64]{0:T(512)(128)(4,1)S(1)} %get-tuple-element.841), kind=kLoop, calls=%fused_computation.91 | loop fusion | flops 8388608 | bytes 33554560 | tf_op jit(solution)/shard_map/jit(_take)/select_n | solution.py:149
  257.8 22.9 %copy.71 = bf16[16,64,64,64]{2,1,3,0:T(8,128)(2,1)} copy(bf16[16,64,64,64]{3,2,0,1:T(8,128)(2,1)} %get-tuple-element.870) | data formatting | bytes 16777216 | tf_op jit(solution)/shard_map/jit(_take)/select_n | solution.py:149
  280.6 22.6 %reshape.403 = bf16[16,4096,64]{1,2,0:T(8,128)(2,1)} reshape(bf16[16,64,64,64]{2,1,3,0:T(8,128)(2,1)} %copy.71) | data formatting | bytes 16777216 | tf_op jit(solution)/shard_map/reshape | solution.py:149
  303.2 60.4 %while.74 = (s32[]{:T(128)}, f32[8,192]{1,0:T(8,128)S(1)}, f32[8,192]{1,0:T(8,128)S(1)}, f32[8,192,64]{1,2,0:T(8,128)}, s32[4096]{0:T(1024)S(1)}, /*index=5*/bf1...) while((s32[]{:T(128)}, f32[8,192]{1,0:T(8,128)S(1)}, ...), condition=%wide.region_5.7_spmd.clone, body=%wide.region_2.6_spmd.clone.sunk | while | flops 423599616 | bytes 24100308 | solution.py:66
  303.5 5.2 fusion.210
  308.7 3.9 fusion.211
  312.6 5.6 fusion.213
  318.5 5.2 fusion.210
  323.7 3.9 fusion.211
  327.6 5.7 fusion.213
  333.6 5.2 fusion.210
  338.9 3.9 fusion.211
  342.8 5.7 fusion.213
  348.8 5.2 fusion.210
  354.0 3.9 fusion.211
  357.9 5.7 fusion.213
  363.6 27.0 %while.72 = (s32[]{:T(128)}, f32[8,192]{1,0:T(8,128)S(1)}, f32[8,192]{1,0:T(8,128)S(1)}, f32[8,192,64]{1,2,0:T(8,128)}, s32[2048]{0:T(1024)S(1)}, /*index=5*/bf1...) while((s32[]{:T(128)}, f32[8,192]{1,0:T(8,128)S(1)}, ...), condition=%wide.region_9.11_spmd.clone, body=%wide.region_6.10_spmd.clone.sunk | while | flops 423496704 | bytes 49266148 | solution.py:66
  371.5 5.7 fusion.200
  384.9 5.7 fusion.200
  391.3 22.9 %copy.79 = bf16[16,64,64,64]{2,1,3,0:T(8,128)(2,1)} copy(bf16[16,64,64,64]{3,2,0,1:T(8,128)(2,1)} %get-tuple-element.869) | data formatting | bytes 16777216 | tf_op jit(solution)/shard_map/jit(_take)/select_n | solution.py:149
  414.1 22.6 %reshape.407 = bf16[16,4096,64]{1,2,0:T(8,128)(2,1)} reshape(bf16[16,64,64,64]{2,1,3,0:T(8,128)(2,1)} %copy.79) | data formatting | bytes 16777216 | tf_op jit(solution)/shard_map/reshape | solution.py:149
  436.8 63.1 %while.75 = (s32[]{:T(128)}, f32[8,192]{1,0:T(8,128)S(1)}, f32[8,192]{1,0:T(8,128)S(1)}, f32[8,192,64]{1,2,0:T(8,128)}, s32[4096]{0:T(1024)}, /*index=5*/bf16[16...) while((s32[]{:T(128)}, f32[8,192]{1,0:T(8,128)S(1)}, ...), condition=%wide.region_13.15_spmd.clone, body=%wide.region_10.14_spmd.clone.sunk | while | flops 423599616 | bytes 24100308 | solution.py:66
  437.7 5.2 fusion.217
  442.9 3.9 fusion.218
  446.9 5.6 fusion.220
  453.4 5.2 fusion.217
  458.6 3.9 fusion.218
  462.5 5.7 fusion.220
  469.2 5.2 fusion.217
  474.4 3.9 fusion.218
  478.3 5.7 fusion.220
  485.0 5.2 fusion.217
  490.2 3.9 fusion.218
  494.1 5.7 fusion.220
  499.8 27.2 %while.73 = (s32[]{:T(128)}, f32[8,192]{1,0:T(8,128)S(1)}, f32[8,192]{1,0:T(8,128)S(1)}, f32[8,192,64]{1,2,0:T(8,128)}, s32[2048]{0:T(1024)S(1)}, /*index=5*/bf1...) while((s32[]{:T(128)}, f32[8,192]{1,0:T(8,128)S(1)}, ...), condition=%wide.region_17.19_spmd.clone, body=%wide.region_14.18_spmd.clone.sunk | while | flops 423496704 | bytes 49266148 | solution.py:66
  507.9 5.7 fusion.206
  521.3 5.7 fusion.206
  532.8 2.7 fusion.105
  535.6 3.1 copy.84
  538.6 2.8 reshape.408
  541.4 3.4 fusion.96
  545.8 6.2 gather_fusion
  552.0 2.8 select_select_fusion
  554.7 62.1 %all_to_all.20 = bf16[32,48,1536]{2,1,0:T(8,128)(2,1)S(1)} all-to-all(bf16[32,48,1536]{2,1,0:T(8,128)(2,1)S(1)} %select_select_fusion), channel_id=1, replica_groups=mesh['req'=4,'tok'=32] {'tok'}, dimensions={0} | all-to-all | bytes 9437184 | tf_op jit(solution)/shard_map/all_to_all | solution.py:210
  616.8 5.4 convolution_bitcast_fusion
  622.3 2.9 fusion.78
  646.6 5.0 all-to-all-start.2
  652.3 59.0 %all-to-all-done.2 = bf16[32,1,48,1536]{3,2,1,0:T(8,128)(2,1)} async-done(((bf16[32,1,48,1536]{3,2,1,0:T(8,128)(2,1)}), bf16[32,1,48,1536]{3,2,1,0:T(8,128)(2,1)}, u32[]{:S(2)}, u32[]{:S(2)}) %all-to-all-start.2) | async-done | bytes 4718624 | tf_op jit(solution)/shard_map/all_to_all | solution.py:20
  711.4 10.2 %gather_fusion.1 = bf16[1024,1536]{1,0:T(8,128)(2,1)} fusion(bf16[1536,1536]{1,0:T(8,128)(2,1)} %bitcast.67, s32[1024]{0:T(1024)S(1)} %broadcast_clamp_fusion), kind=kCustom, calls=%fused_computation.3 | custom fusion | bytes 6295552 | tf_op jit(solution)/shard_map/jit(_take)/gather | solution.py:217
  721.6 2.9 fusion.80
  (256 shorter events, 104.6 us)
Async XLA Ops:
  7.2 609.7 %copy-start = (bf16[1,1536,1024]{2,1,0:T(8,128)(2,1)S(1)}, bf16[1,1536,1024]{2,1,0:T(8,128)(2,1)}, u32[]{:S(2)}) copy-start(bf16[1,1536,1024]{2,1,0:T(8,128)(2,1)} %param.36) | copy-start | bytes 9437188
  7.2 4.8 copy-start.24
  7.2 94.5 %all-gather.5.cloned.1.call-start = ((), (), s32[]{:S(2)}) async-start(), calls=%async_computation.4 | async-start | bytes 8650752 | tf_op jit(solution)/shard_map/all_gather | solution.py:163
  12.0 130.0 %all-gather.3.cloned.1.call-start = ((), (), s32[]{:S(2)}) async-start(), calls=%async_computation.3 | async-start | bytes 17301504 | tf_op jit(solution)/shard_map/all_gather | solution.py:143
  21.8 41.8 %copy-start.3 = (bf16[2,64,1536]{2,1,0:T(8,128)(2,1)S(1)}, bf16[2,64,1536]{2,1,0:T(8,128)(2,1)}, u32[]{:S(2)}) copy-start(bf16[2,64,1536]{2,1,0:T(8,128)(2,1)} %param.24) | copy-start | bytes 1179652
  86.5 27.6 %copy-start.12 = (s32[2,512]{1,0:T(2,128)}, s32[2,512]{1,0:T(2,128)S(1)}, u32[]{:S(2)}) copy-start(s32[2,512]{1,0:T(2,128)S(1)} %fusion.143) | copy-start | bytes 12292
  87.3 26.9 %copy-start.9 = (s32[2,64,8]{1,2,0:T(8,128)}, s32[2,64,8]{1,2,0:T(8,128)S(1)}, u32[]{:S(2)}) copy-start(s32[2,64,8]{1,2,0:T(8,128)S(1)} %broadcast_multiply_fusion) | copy-start | bytes 12292
  87.5 0.6 copy-start.21
  88.2 26.0 %copy-start.17 = (s32[1024,1]{0,1:T(1,128)}, s32[1024,1]{0,1:T(1,128)S(1)}, u32[]{:S(2)}) copy-start(s32[1024,1]{0,1:T(1,128)S(1)} %compare_select_fusion) | copy-start | bytes 12292
  366.8 2.7 copy-start.1
  380.1 2.7 copy-start.1
  414.1 22.6 %copy-start.6 = (f32[8,192]{1,0:T(8,128)S(1)}, f32[8,192]{1,0:T(8,128)}, u32[]{:S(2)}) copy-start(f32[8,192]{1,0:T(8,128)} %custom-call.3) | copy-start | bytes 18436
  414.1 22.6 %copy-start.7 = (f32[8,192]{1,0:T(8,128)S(1)}, f32[8,192]{1,0:T(8,128)}, u32[]{:S(2)}) copy-start(f32[8,192]{1,0:T(8,128)} %custom-call.4) | copy-start | bytes 18436
  414.1 22.6 %copy-start.11 = (s32[64]{0:T(128)S(1)}, s32[64]{0:T(128)}, u32[]{:S(2)}) copy-start(s32[64]{0:T(128)} %get-tuple-element.1145) | copy-start | bytes 772
  436.7 63.1 %copy-start.8 = (s32[2048]{0:T(1024)S(1)}, s32[2048]{0:T(1024)}, u32[]{:S(2)}) copy-start(s32[2048]{0:T(1024)} %iota_add_fusion) | copy-start | bytes 24580
  503.1 2.7 copy-start.2
  516.5 2.7 copy-start.2
  527.0 14.4 %copy-start.4 = (bf16[2,64,1536]{2,1,0:T(8,128)(2,1)S(1)}, bf16[2,64,1536]{2,1,0:T(8,128)(2,1)}, u32[]{:S(2)}) copy-start(bf16[2,64,1536]{2,1,0:T(8,128)(2,1)} %param.24) | copy-start | bytes 1179652
  535.6 9.2 %copy-start.19 = (f32[1536]{0:T(1024)S(1)}, f32[1536]{0:T(1024)}, u32[]{:S(2)}) copy-start(f32[1536]{0:T(1024)} %param.33) | copy-start | bytes 18436
  538.6 7.1 copy-start.14
  541.4 3.4 copy-start.5
  545.8 6.2 copy-start.15
  545.8 6.2 copy-start.16
  616.8 5.4 copy-start.23
  646.6 5.0 copy-start.13
  646.6 5.1 copy-start.10
  646.6 5.3 copy-start.22
  646.6 5.6 copy-start.20
  646.6 5.7 copy-start.18
  646.6 64.8 %all-to-all-start.2 = ((bf16[32,1,48,1536]{3,2,1,0:T(8,128)(2,1)}), bf16[32,1,48,1536]{3,2,1,0:T(8,128)(2,1)}, u32[]{:S(2)}, u32[]{:S(2)}) async-start(bf16[32,1,48,1536]{3,2,1,0:T(8,128)(2,1)} %fusion.110), calls=%async_computation.2 | async-start | bytes 9437184 | tf_op jit(solution)/shard_map/all_to_all | solution.py:20
Sparse Core Ops, SparseCore 0:
  12.1 55.4 all-gather.4
  69.9 72.0 all-gather.2
